TPU v7x, 32 devices: a whole 2x2x4 slice. The times are simulated.
32 devices in a mesh: ctx: 8 (over z, y), mp: 4 (over x, core).
Axes of the slice: x: 2, y: 2, z: 4, core: 2. Of those that a mesh axis runs over, the one named last changes fastest.
Arguments:
- tokens: bfloat16 [3072, 6144], P('ctx', 'mp'), may hold values from -24 to 24, as said below
- qkv_weight: bfloat16 [6144, 3, 24, 128], P('ctx', None, 'mp'), may hold values from -1 to 1, as said below
Outputs:
- attended: bfloat16 [3072, 24, 128], P('ctx', 'mp')
Inputs may be any that keep to these rules, and one draw needn't show every extreme that they name: `tokens`: finite values. `qkv_weight`: entries lie within 8 / sqrt(6144) of zero.
All inputs are finite; a program needn't handle non-finite values.
Results may differ from a plain program's by a relative error of at most 0.0045.
The roundings to bfloat16 on the way count: a program that leaves them out, or rounds other values in their place, can miss the bound.
Values may be sent and summed in bfloat16 or wider, within the bound.
No kernel may reach another device: no remote copies, remote signals or barrier semaphores. Data moves between devices by JAX's collectives and lax.ppermute only.
A program may use at most 128 MiB of HBM per device.

v0:
```python
import math
import jax
import jax.numpy as jnp
from jax import lax
from jax.sharding import PartitionSpec as P

REACH = 4


def shifted(array, axis, by):
    devices = lax.axis_size(axis)
    return lax.ppermute(array, axis, [(i, (i + by) % devices) for i in range(devices)])


def collect_blocks(key_value):
    blocks = [key_value]
    current = key_value
    for step in range(1, REACH):
        current = shifted(current, "ctx", 1)
        blocks.append(current)
    return blocks


def on_device(tokens, qkv_weight):
    features = lax.all_gather(tokens, "mp", axis=1, tiled=True)
    rows_dev = features.shape[0]
    heads_local = qkv_weight.shape[2]
    head_size = qkv_weight.shape[3]
    scale = 1.0 / math.sqrt(head_size)
    piece = lax.all_gather(qkv_weight, "ctx", axis=0, tiled=True)
    flat_piece = piece.reshape(piece.shape[0], -1)
    full_total = jnp.dot(features, flat_piece, preferred_element_type=jnp.float32)
    projected = full_total.astype(jnp.bfloat16).reshape(rows_dev, 3, heads_local, head_size)
    queries = projected[:, 0]
    key_value = projected[:, 1:]
    blocks = collect_blocks(key_value)
    key_rows = jnp.concatenate([block[:, 0] for block in blocks], axis=0)
    value_rows = jnp.concatenate([block[:, 1] for block in blocks], axis=0)
    scores = (
        jnp.einsum("thd,shd->hts", queries, key_rows, preferred_element_type=jnp.float32) * scale
    )
    top = jnp.max(scores, axis=-1, keepdims=True)
    expo = jnp.exp(scores - top)
    totals = jnp.sum(expo, axis=-1, keepdims=True)
    probs = expo.astype(jnp.bfloat16)
    mixed = (
        jnp.einsum("hts,shd->htd", probs, value_rows, preferred_element_type=jnp.float32) / totals
    )
    return jnp.transpose(mixed, (1, 0, 2)).astype(jnp.bfloat16)


def solution(mesh):
    placed = (P("ctx", "mp"), P("ctx", None, "mp", None))
    return jax.shard_map(
        on_device, mesh=mesh, in_specs=placed, out_specs=P("ctx", "mp", None), check_vma=False
    )
```

profile of v0, /device:TPU:0, one launch (start us, length us, event | category | flops | bytes accessed | tf_op | source)
XLA Modules:
  0.0 727.5 jit_solution(14110665750935580521)
XLA Ops:
  6.5 0.0 all-gather.3.cloned.1.call-start
  6.5 0.7 all-gather.3.cloned.1.call-update
  7.3 0.0 all-gather.5.cloned.1.call-start
  7.3 6.1 copy.7
  13.4 0.0 all-gather.5.cloned.1.call-update
  13.4 35.7 %all-gather.3.cloned.1.call-done = bf16[384,6144]{1,0:T(8,128)(2,1)} async-done(((bf16[384,1536]{1,0:T(8,128)(2,1)}), bf16[384,6144]{1,0:T(8,128)(2,1)}) %all-gather.3.cloned.1.call-update) | async-done | bytes 4718608 | tf_op jit(solution)/shard_map/all_gather | solution.py:25
  49.1 541.0 %all-gather.5.cloned.1.call-done = bf16[6144,3,6,128]{0,3,2,1:T(8,128)(2,1)} async-done(((bf16[768,3,6,128]{0,3,2,1:T(8,128)(2,1)}), bf16[6144,3,6,128]{0,3,2,1:T(8,128)(2,1)}) %all-gather.5.cloned.1.call-update) | async-done | bytes 28311568 | tf_op jit(solution)/shard_map/all_gather | solution.py:30
  590.1 16.6 %convolution_convert_fusion = bf16[384,2304]{1,0:T(8,128)(2,1)S(1)} fusion(bf16[384,6144]{1,0:T(8,128)(2,1)} %all-gather.3.cloned.1.call-done, bf16[6144,2304]{0,1:T(8,128)(2,1)} %bitcast.35), kind=kOutput, calls=%fused_computation.7 | convolution fusion | flops 10872520704 | bytes 34799616 | tf_op jit(solution)/shard_map/dot_general | solution.py:32
  606.7 1.1 copy.8
  607.8 0.1 slice.44
  608.0 1.5 copy.15
  609.4 0.3 collective-permute-start
  609.8 30.3 %collective-permute-done = bf16[384,2,6,128]{3,0,2,1:T(8,128)(2,1)S(1)} collective-permute-done((bf16[384,2,6,128]{3,0,2,1:T(8,128)(2,1)}, bf16[384,2,6,128]{3,0,2,1:T(8,128)(2,1)S(1)}, u32[]{:S(2)}, u32[]{:S(2)}) %collective-permute-start) | collective-permute-done | bytes 1179680 | tf_op jit(solution)/shard_map/ppermute | solution.py:12
  640.0 0.0 copy-start
  640.0 0.0 collective-permute-start.1
  640.0 29.6 %collective-permute-done.1 = bf16[384,2,6,128]{3,0,2,1:T(8,128)(2,1)} collective-permute-done((bf16[384,2,6,128]{3,0,2,1:T(8,128)(2,1)S(1)}, bf16[384,2,6,128]{3,0,2,1:T(8,128)(2,1)}, u32[]{:S(2)}, u32[]{:S(2)}) %collective-permute-start.1) | collective-permute-done | bytes 1179680 | tf_op jit(solution)/shard_map/ppermute | solution.py:12
  669.7 0.0 copy-done
  669.7 0.0 collective-permute-start.2
  669.7 0.1 fusion.33
  669.8 0.3 copy.14
  670.1 0.3 copy.16
  670.4 1.3 slice_bitcast_fusion.5
  671.8 1.3 slice_bitcast_fusion.4
  673.1 25.5 %collective-permute-done.2 = bf16[384,2,6,128]{3,0,2,1:T(8,128)(2,1)} collective-permute-done((bf16[384,2,6,128]{3,0,2,1:T(8,128)(2,1)}, bf16[384,2,6,128]{3,0,2,1:T(8,128)(2,1)}, u32[]{:S(2)}, u32[]{:S(2)}) %collective-permute-start.2) | collective-permute-done | bytes 1179680 | tf_op jit(solution)/shard_map/ppermute | solution.py:12
  698.6 1.3 slice_bitcast_fusion.3
  699.9 6.2 multiply_reduce_fusion
  706.1 7.5 %fusion = f32[6,384]{1,0:T(8,128)S(1)} fusion(f32[6,384,1536]{2,1,0:T(8,128)} %get-tuple-element.14, f32[6,384]{1,0:T(8,128)S(1)} %get-tuple-element.13), kind=kLoop, calls=%fused_computation.2 | loop fusion | flops 10614528 | bytes 14174208 | tf_op jit(solution)/shard_map/reduce_sum | solution.py:44
  713.6 7.1 divide_convert_fusion
Async XLA Ops:
  6.5 42.6 %all-gather.3.cloned.1.call-start = ((), (), s32[]{:S(2)}) async-start(), calls=%async_computation | async-start | bytes 5898240 | tf_op jit(solution)/shard_map/all_gather | solution.py:25
  7.3 582.8 %all-gather.5.cloned.1.call-start = ((), (), s32[]{:S(2)}) async-start(), calls=%async_computation.1 | async-start | bytes 31850496 | tf_op jit(solution)/shard_map/all_gather | solution.py:30
  609.4 30.6 %collective-permute-start = (bf16[384,2,6,128]{3,0,2,1:T(8,128)(2,1)}, bf16[384,2,6,128]{3,0,2,1:T(8,128)(2,1)S(1)}, u32[]{:S(2)}, u32[]{:S(2)}) collective-permute-start(bf16[384,2,6,128]{3,0,2,1:T(8,128)(2,1)} %copy.15), channel_id=1, source_target_pairs={{0,4},{4,8},{8,12},{12,16},{16,20},{20,24},{24,28},{28,0},{1,5},{5... | collective-permute-start | bytes 3538952 | tf_op jit(solution)/shard_map/ppermute | solution.py:12
  640.0 29.6 %copy-start = (bf16[384,2,6,128]{3,0,2,1:T(8,128)(2,1)}, bf16[384,2,6,128]{3,0,2,1:T(8,128)(2,1)S(1)}, u32[]{:S(2)}) copy-start(bf16[384,2,6,128]{3,0,2,1:T(8,128)(2,1)S(1)} %collective-permute-done) | copy-start | bytes 3538948
  640.0 29.6 %collective-permute-start.1 = (bf16[384,2,6,128]{3,0,2,1:T(8,128)(2,1)S(1)}, bf16[384,2,6,128]{3,0,2,1:T(8,128)(2,1)}, u32[]{:S(2)}, u32[]{:S(2)}) collective-permute-start(bf16[384,2,6,128]{3,0,2,1:T(8,128)(2,1)S(1)} %collective-permute-done), channel_id=1, source_target_pairs={{0,4},{4,8},{8,12},{12,16},{16,20},{20,24},{24,28},{28,0},{1,5},{5... | collective-permute-start | bytes 3538952 | tf_op jit(solution)/shard_map/ppermute | solution.py:12
  669.7 28.9 %collective-permute-start.2 = (bf16[384,2,6,128]{3,0,2,1:T(8,128)(2,1)}, bf16[384,2,6,128]{3,0,2,1:T(8,128)(2,1)}, u32[]{:S(2)}, u32[]{:S(2)}) collective-permute-start(bf16[384,2,6,128]{3,0,2,1:T(8,128)(2,1)} %collective-permute-done.1), channel_id=1, source_target_pairs={{0,4},{4,8},{8,12},{12,16},{16,20},{20,24},{24,28},{28,0},{1,5},{5... | collective-permute-start | bytes 3538952 | tf_op jit(solution)/shard_map/ppermute | solution.py:12
Sparse Core Ops, SparseCore 0:
  8.9 40.1 all-gather.2
  50.6 539.4 all-gather.4
where the time goes:
time: 728 us
  waiting for transfers between devices  663 us (91%)
  matrix products  29.9 us (4%)
  local copies, waits for them, and re-layouts  13.4 us (2%)
  between operations  13.4 us (2%)
  other arithmetic  7.47 us (1%)
    all_gather x1, waiting for transfers between devices, on_device(): piece = lax.all_gather(qkv_weight, 'ctx', axis=0, tiled=True)  541 us
    ppermute x3, waiting for transfers between devices, shifted(): lax.ppermute(array, axis, [(i, (i + by) % devices) for i in range(devices)])  85.4 us
    all_gather x1, waiting for transfers between devices, on_device(): features = lax.all_gather(tokens, 'mp', axis=1, tiled=True)  35.7 us
    dot_general x1, matrix products, on_device(): jnp.dot(features, flat_piece, preferred_element_type=jnp.float32)  16.6 us
  transfers between devices with their start and end apart: 5, of which 5 were waited for; matrix products, arithmetic and copies ran while one was open for 1% of the time, Pallas kernels for 0%

commit v1 on v0

--- a/solution.py
+++ b/solution.py
@@ -5,6 +5,27 @@
 from jax.sharding import PartitionSpec as P
 
 REACH = 4
+
+
+def laid_out(blocks, dim):
+    blocks = jnp.moveaxis(blocks, 0, dim)
+    dims = blocks.shape
+    return blocks.reshape(*dims[:dim], dims[dim] * dims[dim + 1], *dims[dim + 2 :])
+
+
+def grow_blocks(array, axis):
+    size, index = (lax.axis_size(axis), lax.axis_index(axis))
+    blocks, bit = (array[None], 1)
+    while bit < size:
+        other = lax.ppermute(blocks, axis, [(i, i ^ bit) for i in range(size)])
+        low = index & bit == 0
+        blocks = jnp.concatenate([jnp.where(low, blocks, other), jnp.where(low, other, blocks)])
+        bit *= 2
+    return blocks
+
+
+def gather_by_bits(array, axis, dim):
+    return laid_out(grow_blocks(array, axis), dim)
 
 
 def shifted(array, axis, by):
@@ -22,7 +43,7 @@
 
 
 def on_device(tokens, qkv_weight):
-    features = lax.all_gather(tokens, "mp", axis=1, tiled=True)
+    features = gather_by_bits(tokens, "mp", 1)
     rows_dev = features.shape[0]
     heads_local = qkv_weight.shape[2]
     head_size = qkv_weight.shape[3]

time: 728 us -> 693 us (0.952)
  waiting for transfers between devices: 663 us -> 614 us
  other arithmetic: 7.47 us -> 15.7 us
    all_gather x1, waiting for transfers between devices: 541 us -> 474 us  [on_device(): piece = lax.all_gather(qkv_weight, 'ctx', axis=0, tiled=True)]
    ppermute x0 -> x2, waiting for transfers between devices: none -> 54.5 us  [grow_blocks(): other = lax.ppermute(blocks, axis, [(i, i ^ bit) for i in range(size)])]
    all_gather x1 -> x0, waiting for transfers between devices: 35.7 us -> none  [on_device(): features = lax.all_gather(tokens, 'mp', axis=1, tiled=True)]
  transfers between devices with their start and end apart: 5 -> 6, of which waited for: 5 -> 6; matrix products, arithmetic and copies ran while one was open for 1% -> 2% of each run, Pallas kernels for 0% -> 0%
where the time goes in v1:
time: 693 us; the launch traced here: 692 us
  waiting for transfers between devices  614 us (89%)
  matrix products  30 us (4%)
  other arithmetic  15.7 us (2%)
  local copies, waits for them, and re-layouts  15.4 us (2%)
  between operations  13.5 us (2%)
    all_gather x1, waiting for transfers between devices, on_device(): piece = lax.all_gather(qkv_weight, 'ctx', axis=0, tiled=True)  474 us
    ppermute x3, waiting for transfers between devices, shifted(): lax.ppermute(array, axis, [(i, (i + by) % devices) for i in range(devices)])  85.4 us
    ppermute x2, waiting for transfers between devices, grow_blocks(): other = lax.ppermute(blocks, axis, [(i, i ^ bit) for i in range(size)])  54.5 us
    dot_general x1, matrix products, on_device(): jnp.dot(features, flat_piece, preferred_element_type=jnp.float32)  16.7 us
  transfers between devices with their start and end apart: 6, of which 6 were waited for; matrix products, arithmetic and copies ran while one was open for 2% of the time, Pallas kernels for 0%

profile of v1, /device:TPU:0, one launch (start us, length us, event | category | flops | bytes accessed | tf_op | source)
XLA Modules:
  0.0 692.4 jit_solution(10433217163929893718)
XLA Ops:
  6.5 0.0 all-gather.2.cloned.1.call-start
  6.5 6.1 copy.8
  12.6 0.0 copy-start
  12.6 0.0 all-gather.2.cloned.1.call-update
  12.6 1.2 copy-done
  13.9 0.7 copy.7
  14.6 0.5 collective-permute-start
  15.1 2.6 collective-permute-done
  17.7 1.5 broadcast_select_fusion.3
  19.2 1.8 pad_maximum_fusion.1
  21.0 2.9 collective-permute-start.1
  23.9 51.9 %collective-permute-done.1 = bf16[2,384,1536]{1,2,0:T(8,128)(2,1)} collective-permute-done((bf16[2,384,1536]{1,2,0:T(8,128)(2,1)}, bf16[2,384,1536]{1,2,0:T(8,128)(2,1)}, u32[]{:S(2)}, u32[]{:S(2)}) %collective-permute-start.1) | collective-permute-done | bytes 2359328 | tf_op jit(solution)/shard_map/ppermute | solution.py:20
  75.7 2.3 broadcast_select_fusion.1
  78.0 2.7 pad_maximum_fusion
  80.6 474.2 %all-gather.2.cloned.1.call-done = bf16[6144,3,6,128]{0,3,2,1:T(8,128)(2,1)} async-done(((bf16[768,3,6,128]{0,3,2,1:T(8,128)(2,1)}), bf16[6144,3,6,128]{0,3,2,1:T(8,128)(2,1)}) %all-gather.2.cloned.1.call-update) | async-done | bytes 28311568 | tf_op jit(solution)/shard_map/all_gather | solution.py:51
  554.9 16.7 %convolution_convert_fusion = bf16[384,2304]{1,0:T(8,128)(2,1)S(1)} fusion(bf16[384,6144]{0,1:T(8,128)(2,1)} %bitcast.39, bf16[6144,2304]{0,1:T(8,128)(2,1)} %bitcast.43), kind=kOutput, calls=%fused_computation.8 | convolution fusion | flops 10872520704 | bytes 34799616 | tf_op jit(solution)/shard_map/dot_general | solution.py:53
  571.6 1.1 copy.9
  572.7 0.1 slice.44
  572.8 1.4 copy.16
  574.3 0.3 collective-permute-start.2
  574.6 30.3 %collective-permute-done.2 = bf16[384,2,6,128]{3,0,2,1:T(8,128)(2,1)S(1)} collective-permute-done((bf16[384,2,6,128]{3,0,2,1:T(8,128)(2,1)}, bf16[384,2,6,128]{3,0,2,1:T(8,128)(2,1)S(1)}, u32[]{:S(2)}, u32[]{:S(2)}) %collective-permute-start.2) | collective-permute-done | bytes 1179680 | tf_op jit(solution)/shard_map/ppermute | solution.py:33
  604.9 0.0 copy-start.1
  604.9 0.0 collective-permute-start.3
  604.9 29.6 %collective-permute-done.3 = bf16[384,2,6,128]{3,0,2,1:T(8,128)(2,1)} collective-permute-done((bf16[384,2,6,128]{3,0,2,1:T(8,128)(2,1)S(1)}, bf16[384,2,6,128]{3,0,2,1:T(8,128)(2,1)}, u32[]{:S(2)}, u32[]{:S(2)}) %collective-permute-start.3) | collective-permute-done | bytes 1179680 | tf_op jit(solution)/shard_map/ppermute | solution.py:33
  634.5 0.0 copy-done.1
  634.5 0.0 collective-permute-start.4
  634.5 0.1 fusion.33
  634.7 0.3 copy.15
  635.0 0.3 copy.17
  635.3 1.3 slice_bitcast_fusion.5
  636.6 1.3 slice_bitcast_fusion.4
  638.0 25.5 %collective-permute-done.4 = bf16[384,2,6,128]{3,0,2,1:T(8,128)(2,1)} collective-permute-done((bf16[384,2,6,128]{3,0,2,1:T(8,128)(2,1)}, bf16[384,2,6,128]{3,0,2,1:T(8,128)(2,1)}, u32[]{:S(2)}, u32[]{:S(2)}) %collective-permute-start.4) | collective-permute-done | bytes 1179680 | tf_op jit(solution)/shard_map/ppermute | solution.py:33
  663.5 1.3 slice_bitcast_fusion.3
  664.8 6.2 multiply_reduce_fusion
  671.0 7.5 %fusion = f32[6,384]{1,0:T(8,128)S(1)} fusion(f32[6,384,1536]{2,1,0:T(8,128)} %get-tuple-element.18, f32[6,384]{1,0:T(8,128)S(1)} %get-tuple-element.17), kind=kLoop, calls=%fused_computation.2 | loop fusion | flops 10614528 | bytes 14174208 | tf_op jit(solution)/shard_map/reduce_sum | solution.py:65
  678.5 7.1 %divide_convert_fusion = bf16[384,6,128]{2,0,1:T(8,128)(2,1)} fusion(bf16[384,6,128]{2,0,1:T(8,128)(2,1)S(1)} %get-tuple-element.16, bf16[384,6,128]{2,0,1:T(8,128)(2,1)S(1)} %get-tuple-element.14, bf16[384,6,128]{2,0,1:T(8,128)(2,1)S(1)} %get-tuple-element.12, bf16[384,6,128]{2,0,1:T(8,128)(2,1)S(1)} %bitcast.41, f32[6,384,1536]{2,1,0:T(8,128)} %get-tuple-element.18, ...), kind=kOutput, calls=%fused_computation.28 | convolution fusion | flops 926613504 | bytes 17123328 | tf_op jit(solution)/shard_map/hts,shd->htd/dot_general | solution.py:68
Async XLA Ops:
  6.5 548.4 %all-gather.2.cloned.1.call-start = ((), (), s32[]{:S(2)}) async-start(), calls=%async_computation | async-start | bytes 31850496 | tf_op jit(solution)/shard_map/all_gather | solution.py:51
  12.6 1.3 copy-start
  14.6 3.1 collective-permute-start
  21.0 54.7 %collective-permute-start.1 = (bf16[2,384,1536]{1,2,0:T(8,128)(2,1)}, bf16[2,384,1536]{1,2,0:T(8,128)(2,1)}, u32[]{:S(2)}, u32[]{:S(2)}) collective-permute-start(bf16[2,384,1536]{1,2,0:T(8,128)(2,1)} %pad_maximum_fusion.1), channel_id=1, source_target_pairs={{0,2},{1,3},{2,0},{3,1},{4,6},{5,7},{6,4},{7,5},{8,10},{9,11},{10,... | collective-permute-start | bytes 7077896 | tf_op jit(solution)/shard_map/ppermute | solution.py:20
  574.3 30.6 %collective-permute-start.2 = (bf16[384,2,6,128]{3,0,2,1:T(8,128)(2,1)}, bf16[384,2,6,128]{3,0,2,1:T(8,128)(2,1)S(1)}, u32[]{:S(2)}, u32[]{:S(2)}) collective-permute-start(bf16[384,2,6,128]{3,0,2,1:T(8,128)(2,1)} %copy.16), channel_id=1, source_target_pairs={{0,4},{4,8},{8,12},{12,16},{16,20},{20,24},{24,28},{28,0},{1,5},{5... | collective-permute-start | bytes 3538952 | tf_op jit(solution)/shard_map/ppermute | solution.py:33
  604.9 29.6 %copy-start.1 = (bf16[384,2,6,128]{3,0,2,1:T(8,128)(2,1)}, bf16[384,2,6,128]{3,0,2,1:T(8,128)(2,1)S(1)}, u32[]{:S(2)}) copy-start(bf16[384,2,6,128]{3,0,2,1:T(8,128)(2,1)S(1)} %collective-permute-done.2) | copy-start | bytes 3538948
  604.9 29.6 %collective-permute-start.3 = (bf16[384,2,6,128]{3,0,2,1:T(8,128)(2,1)S(1)}, bf16[384,2,6,128]{3,0,2,1:T(8,128)(2,1)}, u32[]{:S(2)}, u32[]{:S(2)}) collective-permute-start(bf16[384,2,6,128]{3,0,2,1:T(8,128)(2,1)S(1)} %collective-permute-done.2), channel_id=1, source_target_pairs={{0,4},{4,8},{8,12},{12,16},{16,20},{20,24},{24,28},{28,0},{1,5},{5... | collective-permute-start | bytes 3538952 | tf_op jit(solution)/shard_map/ppermute | solution.py:33
  634.5 28.9 %collective-permute-start.4 = (bf16[384,2,6,128]{3,0,2,1:T(8,128)(2,1)}, bf16[384,2,6,128]{3,0,2,1:T(8,128)(2,1)}, u32[]{:S(2)}, u32[]{:S(2)}) collective-permute-start(bf16[384,2,6,128]{3,0,2,1:T(8,128)(2,1)} %collective-permute-done.3), channel_id=1, source_target_pairs={{0,4},{4,8},{8,12},{12,16},{16,20},{20,24},{24,28},{28,0},{1,5},{5... | collective-permute-start | bytes 3538952 | tf_op jit(solution)/shard_map/ppermute | solution.py:33
Sparse Core Ops, SparseCore 0:
  12.7 542.1 all-gather.1
